TPU v7x, 32 devices: a whole 2x2x4 slice. The times are simulated.
32 devices in a mesh: ax: 8 (over z, x), rad: 4 (over y, core).
Axes of the slice: x: 2, y: 2, z: 4, core: 2. Of those that a mesh axis runs over, the one named last changes fastest.
Arguments:
- velocity: float32 [3, 12, 24, 768], P(None, 'rad', 'ax'), may hold values from -50 to 50
- cycle_map: int32 [3, 768], replicated, may hold values from 0 to 95, never falling along the last dimension, each value on 1 to 16 neighbouring positions
Outputs:
- new_velocity: float32 [3, 12, 24, 768], P(None, 'rad', 'ax')
Inputs may be any that keep to these rules, and one draw needn't show every extreme that they name: `cycle_map`: in each row the numbers never fall along the azimuth, and each of 0 to 95 is taken by 1 to 16 consecutive points, one by exactly 16.
All inputs are finite; a program needn't handle non-finite values.
Results may differ from a plain program's by a relative error of at most 0.0003.
Values sent between devices are 32-bit elements; how exact they have to be, the bound alone decides.
A program may use at most 64 MiB of HBM per device.

v0:
```python
import jax
import jax.numpy as jnp
from jax import lax
from jax.sharding import PartitionSpec as P

NRING = 3
NC = 96


COMPONENT_PAIRS = ((0, 0), (1, 1), (2, 2), (0, 1), (0, 2), (1, 2))
PAIR_WEIGHTS = (1.0, 1.0, 1.0, 2.0, 2.0, 2.0)
VECTOR_SIGNS = (1.0, -1.0, -1.0)
RADIAL_FLUX_SIGNS = (-1.0, 1.0, 1.0)
ORDERED_PAIRS = (0, 4, 3, 1, 5, 2)
AXIAL_SLOTS = (0, 2, 1)
AZIMUTH_SLOTS = (1, 4, 5)
time_step = 1.0
epsilon = 1e-06


def with_halo(cells, sides, width, closed):
    for axis, dim in sides:
        count = lax.axis_size(axis)
        ends = count if closed else count - 1
        head = lax.slice_in_dim(cells, 0, width, axis=dim)
        tail = lax.slice_in_dim(cells, cells.shape[dim] - width, cells.shape[dim], axis=dim)
        cells = jnp.concatenate(
            [
                lax.ppermute(tail, axis, [(i, (i + 1) % count) for i in range(ends)]),
                cells,
                lax.ppermute(head, axis, [((i + 1) % count, i) for i in range(ends)]),
            ],
            axis=dim,
        )
    return cells


def trimmed(quantity, margin):
    return quantity[margin:-margin, margin:-margin]


def central(quantity, direction):
    if direction == 0:
        return (quantity[1:-1, 2:] - quantity[1:-1, :-2]) * 0.5
    if direction == 1:
        return (quantity[2:, 1:-1] - quantity[:-2, 1:-1]) * 0.5
    shifted = (jnp.roll(quantity, -1, 2) - jnp.roll(quantity, 1, 2)) * 0.5
    return shifted[1:-1, 1:-1]


def test_filter(quantity):
    along_axis = (quantity[1:-1, :-2] + 2.0 * quantity[1:-1, 1:-1] + quantity[1:-1, 2:]) * 0.25
    return (jnp.roll(along_axis, 1, 2) + 2.0 * along_axis + jnp.roll(along_axis, -1, 2)) * 0.25


def strain_rate(velocity):
    gradient = [
        [central(velocity[component], direction) for direction in range(3)]
        for component in range(3)
    ]
    tensor = [
        0.5 * (gradient[left_index][right_index] + gradient[right_index][left_index])
        for left_index, right_index in COMPONENT_PAIRS
    ]
    squares = sum((weight * member * member for weight, member in zip(PAIR_WEIGHTS, tensor)))
    return (tensor, jnp.sqrt(2.0 * squares))


def model_terms(velocity):
    tensor, magnitude = strain_rate(velocity)
    filtered = [test_filter(component) for component in velocity]
    tensor_hat, magnitude_hat = strain_rate(filtered)
    leonard_model = 0.0
    model_model = 0.0
    for number, (left_index, right_index) in enumerate(COMPONENT_PAIRS):
        product_hat = trimmed(test_filter(velocity[left_index] * velocity[right_index]), 1)
        leonard = product_hat - trimmed(filtered[left_index], 1) * trimmed(filtered[right_index], 1)
        model_term = (
            test_filter(magnitude * tensor[number]) - 4.0 * magnitude_hat * tensor_hat[number]
        )
        leonard_model = leonard_model + PAIR_WEIGHTS[number] * leonard * model_term
        model_model = model_model + PAIR_WEIGHTS[number] * model_term * model_term
    return (leonard_model, model_model, tensor, magnitude)


def flux_terms(velocity, tensor, magnitude, coefficient, margin_in, margin_out):
    speed_trim = margin_in - margin_out
    stress_trim = margin_in - 1 - margin_out
    viscosity = 2.0 * coefficient[:, None, None] * trimmed(magnitude, stress_trim)
    fluxes = []
    for number, (left_index, right_index) in enumerate(COMPONENT_PAIRS):
        advected = trimmed(velocity[left_index], speed_trim) * trimmed(
            velocity[right_index], speed_trim
        )
        fluxes.append(advected - viscosity * trimmed(tensor[number], stress_trim))
    return fluxes


def radial_rims(extended, rim_depth, rad_index, rad_count, sign_values):
    sign_column = jnp.asarray(sign_values, extended.dtype)[:, None, None, None]
    half_turn = extended.shape[3] // 2
    mirrored = sign_column * jnp.roll(extended[:, rim_depth : 2 * rim_depth][:, ::-1], half_turn, 3)
    inner_rows = jnp.where(rad_index == 0, mirrored, extended[:, :rim_depth])
    outer_rows = jnp.where(rad_index == rad_count - 1, 0.0, extended[:, -rim_depth:])
    return jnp.concatenate([inner_rows, extended[:, rim_depth:-rim_depth], outer_rows], axis=1)


def coarsen_cycles(velocity, cycle_map):
    labels = jnp.arange(NC, dtype=jnp.int32)
    theta_points = velocity.shape[3]
    cycle_list = []
    for cycle_number in range(NRING):
        one_hot = (cycle_map[cycle_number][:, None] == labels[None, :]).astype(jnp.float32)
        cell_count = jnp.sum(one_hot, axis=0)
        cycle_rows = velocity[:, cycle_number].reshape(-1, theta_points)
        cycle_sums = jnp.dot(
            cycle_rows, one_hot, precision=lax.Precision.HIGHEST, preferred_element_type=jnp.float32
        )
        cycle_means = cycle_sums / cell_count
        spread = jnp.dot(
            cycle_means,
            one_hot.T,
            precision=lax.Precision.HIGHEST,
            preferred_element_type=jnp.float32,
        )
        cycle_list.append(spread.reshape(velocity[:, cycle_number].shape))
    return jnp.concatenate([jnp.stack(cycle_list, axis=1), velocity[:, NRING:]], axis=1)


def shards(velocity, cycle_map):
    rad_index = lax.axis_index("rad")
    rad_count = lax.axis_size("rad")
    coarse = lax.cond(
        rad_index == 0,
        lambda values: coarsen_cycles(values, cycle_map),
        lambda values: values,
        velocity,
    )
    rim_depth = 2
    padded = with_halo(coarse, (("ax", 2), ("rad", 1)), rim_depth, True)
    padded = radial_rims(padded, rim_depth, rad_index, rad_count, VECTOR_SIGNS)
    components = [padded[0], padded[1], padded[2]]
    cell_count = lax.axis_size("ax") * velocity.shape[2] * velocity.shape[3]
    leonard_model, model_model, tensor, magnitude = model_terms(components)
    lm_rows = jnp.sum(leonard_model, axis=(1, 2))
    mm_rows = jnp.sum(model_model, axis=(1, 2))
    lm_total, mm_total = lax.psum((lm_rows, mm_rows), "ax")
    coefficient = lm_total / cell_count / (mm_total / cell_count + epsilon)
    flux_list = flux_terms(components, tensor, magnitude, coefficient, 2, 0)
    ordered = jnp.stack([flux_list[number] for number in ORDERED_PAIRS])
    axial_part = with_halo(ordered[0:3], (("ax", 2),), 1, True)
    radial_part = with_halo(ordered[2:5], (("rad", 1),), 1, False)
    radial_part = radial_rims(radial_part, 1, rad_index, rad_count, RADIAL_FLUX_SIGNS)
    axial_diff = (axial_part[:, :, 2:] - axial_part[:, :, :-2]) * 0.5
    radial_diff = (radial_part[:, 2:] - radial_part[:, :-2]) * 0.5
    tendencies = []
    for component in range(3):
        beside_all = ordered[AZIMUTH_SLOTS[component]]
        azimuth_diff = (jnp.roll(beside_all, -1, 2) - jnp.roll(beside_all, 1, 2)) * 0.5
        summed = axial_diff[AXIAL_SLOTS[component]] + radial_diff[component]
        summed = summed + azimuth_diff
        tendencies.append(-summed)
    updated = [
        trimmed(components[component], rim_depth) + time_step * tendencies[component]
        for component in range(3)
    ]
    return jnp.stack(updated)


def solution(mesh):
    in_specs = (P(None, "rad", "ax", None), P())
    out_specs = P(None, "rad", "ax", None)
    return jax.shard_map(shards, mesh=mesh, in_specs=in_specs, out_specs=out_specs, check_vma=False)
```

profile of v0, /device:TPU:1, one launch (start us, length us, event | category | flops | bytes accessed | tf_op | source)
XLA Modules:
  0.0 56.9 jit_solution(9671422668862942287)
XLA Ops:
  0.0 0.9 %conditional.1 = (f32[3,3,3,768]{3,2,0,1:T(4,128)S(1)}) conditional(s32[]{:T(128)} %convert_element_type.12, (f32[3,3,3,768]{3,2,1,0:T(4,128)}) %tuple.14, (s32[3,768]{1,0:T(4,128)}, f32[3,3,3,768]{3,2,1,0:T(4,128)}) %tuple.11), branch_computations={%region_0.0_spmd, %region_1.0_spmd} | conditional | flops 48925440 | bytes 898568 | solution.py:133
  0.0 0.9 %copy.20 = f32[3,3,3,768]{3,2,0,1:T(4,128)S(1)} copy(f32[3,3,3,768]{3,2,1,0:T(4,128)} %get-tuple-element.22) | data formatting | bytes 165888 | tf_op args[0]
  1.0 2.1 %collective-permute-start = (f32[3,3,2,768]{3,2,1,0:T(2,128)S(1)}, f32[3,3,2,768]{3,2,1,0:T(2,128)S(1)}, u32[]{:S(2)}, u32[]{:S(2)}) collective-permute-start(f32[3,3,2,768]{3,2,1,0:T(2,128)S(1)} %get-tuple-element.158), channel_id=1, source_target_pairs={{0,4},{4,8},{8,12},{12,16},{16,20},{20,24},{24,28},{28,0},{1,5},{5... | collective-permute-start | bytes 165896 | tf_op jit(solution)/shard_map/ppermute | solution.py:29
  3.1 3.1 %collective-permute-start.1 = (f32[3,3,2,768]{3,2,1,0:T(2,128)S(1)}, f32[3,3,2,768]{3,2,1,0:T(2,128)S(1)}, u32[]{:S(2)}, u32[]{:S(2)}) collective-permute-start(f32[3,3,2,768]{3,2,1,0:T(2,128)S(1)} %get-tuple-element.159), channel_id=1, source_target_pairs={{4,0},{8,4},{12,8},{16,12},{20,16},{24,20},{28,24},{0,28},{5,1},{9... | collective-permute-start | bytes 165896 | tf_op jit(solution)/shard_map/ppermute | solution.py:31
  6.2 1.5 %collective-permute-done = f32[3,3,2,768]{3,2,1,0:T(2,128)S(1)} collective-permute-done((f32[3,3,2,768]{3,2,1,0:T(2,128)S(1)}, f32[3,3,2,768]{3,2,1,0:T(2,128)S(1)}, u32[]{:S(2)}, u32[]{:S(2)}) %collective-permute-start) | collective-permute-done | bytes 55328 | tf_op jit(solution)/shard_map/ppermute | solution.py:29
  7.8 4.2 %collective-permute-start.3 = (f32[3,2,7,768]{3,2,1,0:T(8,128)S(1)}, f32[3,2,7,768]{3,2,1,0:T(8,128)S(1)}, u32[]{:S(2)}, u32[]{:S(2)}) collective-permute-start(f32[3,2,7,768]{3,2,1,0:T(8,128)S(1)} %get-tuple-element.86), channel_id=1, source_target_pairs={{1,0},{2,1},{3,2},{0,3},{5,4},{6,5},{7,6},{4,7},{9,8},{10,9},{11,1... | collective-permute-start | bytes 387080 | tf_op jit(solution)/shard_map/ppermute | solution.py:31
  12.1 1.4 %collective-permute-done.3 = f32[3,2,7,768]{3,2,1,0:T(8,128)S(1)} collective-permute-done((f32[3,2,7,768]{3,2,1,0:T(8,128)S(1)}, f32[3,2,7,768]{3,2,1,0:T(8,128)S(1)}, u32[]{:S(2)}, u32[]{:S(2)}) %collective-permute-start.3) | collective-permute-done | bytes 129056 | tf_op jit(solution)/shard_map/ppermute | solution.py:31
  13.5 2.1 %collective-permute-done.2 = f32[3,2,7,768]{3,2,1,0:T(8,128)S(1)} collective-permute-done((f32[3,2,7,768]{3,2,1,0:T(8,128)S(1)}, f32[3,2,7,768]{3,2,1,0:T(8,128)S(1)}, u32[]{:S(2)}, u32[]{:S(2)}) %collective-permute-start.2) | collective-permute-done | bytes 129056 | tf_op jit(solution)/shard_map/ppermute | solution.py:29
  16.6 0.2 broadcast_multiply_fusion.1
  17.0 0.2 broadcast_multiply_fusion.8
  19.1 0.2 fusion.194
  19.2 0.3 fusion.183
  20.7 0.2 fusion.53
  21.0 0.8 %fusion.167 = (f32[3]{0:T(128)S(1)}, f32[3,3,768]{2,1,0:T(4,128)S(1)}, f32[3,3,768]{2,1,0:T(4,128)S(1)}, f32[3,3,768]{2,1,0:T(4,128)S(1)}, f32[3,3,768]{2,1,0:T(...) fusion(f32[5,5,1]{2,1,0:T(8,128)S(1)} %get-tuple-element.153, f32[5,5,767]{2,1,0:T(8,128)S(1)} %get-tuple-element.155, ...), kind=kLoop, calls=%fused_computation.315 | loop fusion | flops 953853 | bytes 2414604 | tf_op jit(solution)/shard_map/reduce_sum | solution.py:145
  21.8 0.1 fusion.166
  21.9 18.1 %all-reduce = (f32[3]{0:T(128)S(1)}, f32[3]{0:T(128)S(1)}) all-reduce(f32[3]{0:T(128)S(1)} %fusion.166, f32[3]{0:T(128)S(1)} %get-tuple-element.32), channel_id=1, replica_groups=mesh['ax'=8,'rad'=4] {'ax'}, use_global_device_ids=true, to_apply=%region_8.9 | all-reduce | flops 6 | bytes 48 | tf_op jit(solution)/shard_map/psum | solution.py:147
  40.1 0.1 fusion.59
  40.8 8.1 %collective-permute-start.7 = (f32[3,1,3,768]{3,2,1,0:T(4,128)S(1)}, f32[3,1,3,768]{3,2,1,0:T(4,128)S(1)}, u32[]{:S(2)}, u32[]{:S(2)}) collective-permute-start(f32[3,1,3,768]{3,2,1,0:T(4,128)S(1)} %pad_maximum_fusion.23), channel_id=1, source_target_pairs={{0,1},{1,2},{2,3},{4,5},{5,6},{6,7},{8,9},{9,10},{10,11},{12,13},{... | collective-permute-start | bytes 82952 | tf_op jit(solution)/shard_map/ppermute | solution.py:29
  49.1 1.4 %collective-permute-start.5 = (f32[3,3,1,768]{3,2,1,0:T(1,128)S(1)}, f32[3,3,1,768]{3,2,1,0:T(1,128)S(1)}, u32[]{:S(2)}, u32[]{:S(2)}) collective-permute-start(f32[3,3,1,768]{3,2,1,0:T(1,128)S(1)} %get-tuple-element.157), channel_id=1, source_target_pairs={{0,4},{4,8},{8,12},{12,16},{16,20},{20,24},{24,28},{28,0},{1,5},{5... | collective-permute-start | bytes 82952 | tf_op jit(solution)/shard_map/ppermute | solution.py:29
  50.6 1.9 %collective-permute-start.6 = (f32[3,1,3,768]{3,2,1,0:T(4,128)S(1)}, f32[3,1,3,768]{3,2,1,0:T(4,128)S(1)}, u32[]{:S(2)}, u32[]{:S(2)}) collective-permute-start(f32[3,1,3,768]{3,2,1,0:T(4,128)S(1)} %slice.1099), channel_id=1, source_target_pairs={{1,0},{2,1},{3,2},{5,4},{6,5},{7,6},{9,8},{10,9},{11,10},{13,12},{... | collective-permute-start | bytes 82952 | tf_op jit(solution)/shard_map/ppermute | solution.py:31
  52.6 3.2 %collective-permute-done.6 = f32[3,1,3,768]{3,2,1,0:T(4,128)S(1)} collective-permute-done((f32[3,1,3,768]{3,2,1,0:T(4,128)S(1)}, f32[3,1,3,768]{3,2,1,0:T(4,128)S(1)}, u32[]{:S(2)}, u32[]{:S(2)}) %collective-permute-start.6) | collective-permute-done | bytes 27680 | tf_op jit(solution)/shard_map/ppermute | solution.py:31
  55.9 0.1 fusion.45
  56.1 0.1 fusion.74
  56.3 0.7 %pad_maximum_fusion.22 = f32[3,3,3,768]{3,2,1,0:T(4,128)} fusion(f32[1,3,3,768]{3,2,1,0:T(4,128)S(1)} %get-tuple-element.82, f32[1,3,3,768]{3,2,1,0:T(4,128)S(1)} %fusion.69, f32[1,3,3,768]{3,2,1,0:T(4,128)S(1)} %get-tuple-element.81), kind=kLoop, calls=%fused_computation.107 | loop fusion | flops 41472 | bytes 165888 | tf_op jit(solution)/shard_map/stack | solution.py:167
  (87 shorter events, 5.2 us)
Async XLA Ops:
  1.0 6.7 %collective-permute-start = (f32[3,3,2,768]{3,2,1,0:T(2,128)S(1)}, f32[3,3,2,768]{3,2,1,0:T(2,128)S(1)}, u32[]{:S(2)}, u32[]{:S(2)}) collective-permute-start(f32[3,3,2,768]{3,2,1,0:T(2,128)S(1)} %get-tuple-element.158), channel_id=1, source_target_pairs={{0,4},{4,8},{8,12},{12,16},{16,20},{20,24},{24,28},{28,0},{1,5},{5... | collective-permute-start | bytes 165896 | tf_op jit(solution)/shard_map/ppermute | solution.py:29
  3.1 4.6 %collective-permute-start.1 = (f32[3,3,2,768]{3,2,1,0:T(2,128)S(1)}, f32[3,3,2,768]{3,2,1,0:T(2,128)S(1)}, u32[]{:S(2)}, u32[]{:S(2)}) collective-permute-start(f32[3,3,2,768]{3,2,1,0:T(2,128)S(1)} %get-tuple-element.159), channel_id=1, source_target_pairs={{4,0},{8,4},{12,8},{16,12},{20,16},{24,20},{28,24},{0,28},{5,1},{9... | collective-permute-start | bytes 165896 | tf_op jit(solution)/shard_map/ppermute | solution.py:31
  7.8 5.7 %collective-permute-start.3 = (f32[3,2,7,768]{3,2,1,0:T(8,128)S(1)}, f32[3,2,7,768]{3,2,1,0:T(8,128)S(1)}, u32[]{:S(2)}, u32[]{:S(2)}) collective-permute-start(f32[3,2,7,768]{3,2,1,0:T(8,128)S(1)} %get-tuple-element.86), channel_id=1, source_target_pairs={{1,0},{2,1},{3,2},{0,3},{5,4},{6,5},{7,6},{4,7},{9,8},{10,9},{11,1... | collective-permute-start | bytes 387080 | tf_op jit(solution)/shard_map/ppermute | solution.py:31
  12.0 3.7 %copy-start.1 = (f32[3]{0:T(128)S(1)}, f32[3]{0:T(128)}, u32[]{:S(2)}) copy-start(f32[3]{0:T(128)} %constant.63.clone) | copy-start | bytes 40
  12.0 3.6 %collective-permute-start.2 = (f32[3,2,7,768]{3,2,1,0:T(8,128)S(1)}, f32[3,2,7,768]{3,2,1,0:T(8,128)S(1)}, u32[]{:S(2)}, u32[]{:S(2)}) collective-permute-start(f32[3,2,7,768]{3,2,1,0:T(8,128)S(1)} %get-tuple-element.85), channel_id=1, source_target_pairs={{0,1},{1,2},{2,3},{3,0},{4,5},{5,6},{6,7},{7,4},{8,9},{9,10},{10,1... | collective-permute-start | bytes 387080 | tf_op jit(solution)/shard_map/ppermute | solution.py:29
  40.8 11.7 %collective-permute-start.7 = (f32[3,1,3,768]{3,2,1,0:T(4,128)S(1)}, f32[3,1,3,768]{3,2,1,0:T(4,128)S(1)}, u32[]{:S(2)}, u32[]{:S(2)}) collective-permute-start(f32[3,1,3,768]{3,2,1,0:T(4,128)S(1)} %pad_maximum_fusion.23), channel_id=1, source_target_pairs={{0,1},{1,2},{2,3},{4,5},{5,6},{6,7},{8,9},{9,10},{10,11},{12,13},{... | collective-permute-start | bytes 82952 | tf_op jit(solution)/shard_map/ppermute | solution.py:29
  49.0 6.8 %collective-permute-start.4 = (f32[3,3,1,768]{3,2,1,0:T(1,128)S(1)}, f32[3,3,1,768]{3,2,1,0:T(1,128)S(1)}, u32[]{:S(2)}, u32[]{:S(2)}) collective-permute-start(f32[3,3,1,768]{3,2,1,0:T(1,128)S(1)} %get-tuple-element.156), channel_id=1, source_target_pairs={{4,0},{8,4},{12,8},{16,12},{20,16},{24,20},{28,24},{0,28},{5,1},{9... | collective-permute-start | bytes 82952 | tf_op jit(solution)/shard_map/ppermute | solution.py:31
  49.1 3.4 %copy-start = (f32[3]{0:T(128)S(1)}, f32[3]{0:T(128)}, u32[]{:S(2)}) copy-start(f32[3]{0:T(128)} %constant.64.clone) | copy-start | bytes 40
  49.1 6.8 %collective-permute-start.5 = (f32[3,3,1,768]{3,2,1,0:T(1,128)S(1)}, f32[3,3,1,768]{3,2,1,0:T(1,128)S(1)}, u32[]{:S(2)}, u32[]{:S(2)}) collective-permute-start(f32[3,3,1,768]{3,2,1,0:T(1,128)S(1)} %get-tuple-element.157), channel_id=1, source_target_pairs={{0,4},{4,8},{8,12},{12,16},{16,20},{20,24},{24,28},{28,0},{1,5},{5... | collective-permute-start | bytes 82952 | tf_op jit(solution)/shard_map/ppermute | solution.py:29
  50.6 5.3 %collective-permute-start.6 = (f32[3,1,3,768]{3,2,1,0:T(4,128)S(1)}, f32[3,1,3,768]{3,2,1,0:T(4,128)S(1)}, u32[]{:S(2)}, u32[]{:S(2)}) collective-permute-start(f32[3,1,3,768]{3,2,1,0:T(4,128)S(1)} %slice.1099), channel_id=1, source_target_pairs={{1,0},{2,1},{3,2},{5,4},{6,5},{7,6},{9,8},{10,9},{11,10},{13,12},{... | collective-permute-start | bytes 82952 | tf_op jit(solution)/shard_map/ppermute | solution.py:31
where the time goes:
time: 57.2 us; the launch traced here: 56.9 us
  starting transfers between devices  21 us (37%)
  blocking collectives  18.1 us (32%)
  waiting for transfers between devices  8.3 us (15%)
  local copies, waits for them, and re-layouts  4.89 us (9%)
  other arithmetic  4.18 us (7%)
    psum x1, blocking collectives, shards(): lm_total, mm_total = lax.psum((lm_rows, mm_rows), 'ax')  18.1 us
    ppermute x4, starting transfers between devices, with_halo(): lax.ppermute(tail, axis, [(i, (i + 1) % count) for i in range(ends)])  11.7 us
    ppermute x4, starting transfers between devices, with_halo(): lax.ppermute(head, axis, [((i + 1) % count, i) for i in range(ends)])  9.27 us
    ppermute x4, waiting for transfers between devices, with_halo(): lax.ppermute(head, axis, [((i + 1) % count, i) for i in range(ends)])  4.68 us
    ppermute x4, waiting for transfers between devices, with_halo(): lax.ppermute(tail, axis, [(i, (i + 1) % count) for i in range(ends)])  3.62 us
    slice x24, local copies, waits for them, and re-layouts, test_filter(): jnp.roll(along_axis, 1, 2) + 2.0 * along_axis + jnp.roll(along_axis, -1, 2)  1.92 us
  transfers between devices with their start and end apart: 8, of which 4 were waited for; matrix products, arithmetic and copies ran while one was open for 0% of the time, Pallas kernels for 0%

commit v1 on v0

v1 whole, which is shorter than its diff:
```python
import functools

import jax
import jax.numpy as jnp
from jax import lax
from jax.experimental import pallas as pl
from jax.experimental.pallas import tpu as pltpu
from jax.sharding import PartitionSpec as P

NRING = 3
MOSTSEG = 16
SUB = 8
LANES = 128
PAIRS = ((0, 0), (1, 1), (2, 2), (0, 1), (0, 2), (1, 2))
PAIR_WEIGHTS = (1.0, 1.0, 1.0, 2.0, 2.0, 2.0)
SIGNS = (1.0, -1.0, -1.0)
EPSILON = 1e-06
MESH = pl.DeviceIdType.MESH


def pair(a, b):
    return PAIRS.index((min(a, b), max(a, b)))


def each(count, body):
    if count <= 16:
        for i in range(count):
            body(i)
    else:
        lax.fori_loop(0, count, lambda i, c: (body(i), c)[1], 0)


def roll(x, shift, axis):
    size = x.shape[axis]
    return pltpu.roll(x, shift % size, axis)


def up(x):
    return roll(x, -1, x.ndim - 1)


def down(x):
    return roll(x, 1, x.ndim - 1)


def smooth_t(x):
    return (down(x) + 2.0 * x + up(x)) * 0.25


def smooth_z(x):
    return (x[:, :-2] + 2.0 * x[:, 1:-1] + x[:, 2:]) * 0.25


def segments(x, wide, pad):
    rows, total = x.shape
    tiles = total // LANES
    lane = lax.broadcasted_iota(jnp.int32, (rows, LANES), 1)
    pieces = []
    for s in range(SUB):
        start = (s * wide - pad) % total
        k, off = start // LANES, start % LANES
        first = x[:, k * LANES : (k + 1) * LANES]
        if off:
            k2 = (k + 1) % tiles
            second = x[:, k2 * LANES : (k2 + 1) * LANES]
            first = jnp.where(lane < LANES - off, roll(first, -off, 1), roll(second, -off, 1))
        pieces.append(first)
    return pieces


def joined(pieces, wide, pad):
    rows = pieces[0].shape[0]
    lane = lax.broadcasted_iota(jnp.int32, (rows, LANES), 1)
    tiles = []
    for k in range(SUB * wide // LANES):
        lo, hi = k * LANES, (k + 1) * LANES
        s = lo // wide
        out = None
        while s * wide < hi:
            part = roll(pieces[s], s * wide - pad - lo, 1)
            out = part if out is None else jnp.where(lane >= s * wide - lo, part, out)
            s += 1
        tiles.append(out)
    return tiles


def strain(grads):
    tensor = []
    for c, a in PAIRS:
        if c == a:
            tensor.append(0.5 * grads[c][c])
        else:
            tensor.append(0.25 * (grads[c][a] + grads[a][c]))
    squares = sum(w * m * m for w, m in zip(PAIR_WEIGHTS, tensor))
    return tensor, jnp.sqrt(2.0 * squares)


def gradients(f):
    out = []
    for c in range(3):
        mid = f[c][1:-1, 1:-1]
        out.append(
            [
                f[c][1:-1, 2:] - f[c][1:-1, :-2],
                f[c][2:, 1:-1] - f[c][:-2, 1:-1],
                up(mid) - down(mid),
            ]
        )
    return out


def kernel(n_ax, n_rad, v_ref, map_ref, out_ref, own, maps, ext, hx, part, parts, edge_coef,
           halo_send, halo_recv, h_send, h_recv, p_send, p_recv):
    rad = lax.axis_index("rad")
    ax = lax.axis_index("ax")
    R, Z, T = v_ref.shape[1], v_ref.shape[2], v_ref.shape[3]
    wide = T // SUB
    pad = (LANES - wide) // 2
    half = SUB // 2
    right, left = lax.rem(ax + 1, n_ax), lax.rem(ax + n_ax - 1, n_ax)
    has_lo, has_hi = rad > 0, rad < n_rad - 1

    barrier = pltpu.get_barrier_semaphore()

    def greet(to_rad, first):
        def body(i):
            peer = lax.rem(ax + first + i, n_ax)
            pl.semaphore_signal(barrier, inc=1, device_id=(peer, to_rad), device_id_type=MESH)
        each(n_ax - first, body)

    greet(rad, 1)
    pl.when(has_lo)(lambda: greet(rad - 1, 0))
    pl.when(has_hi)(lambda: greet(rad + 1, 0))

    for c in range(3):
        for r in range(R):
            for s, piece in enumerate(segments(v_ref[c, r], wide, pad)):
                own[pl.ds((c * R + r) * Z * SUB + s, Z, stride=SUB), :] = piece
    for c in range(3):
        for r in range(R):
            for z in range(Z):
                row = ((c * R + r) * Z + z) * SUB
                ext[c, r + 1, z + 2] = own[row : row + SUB, :]

    @pl.when(rad == 0)
    def _():
        labels = map_ref[...].astype(jnp.float32)
        for s, piece in enumerate(segments(labels, wide, pad)):
            maps[pl.ds(s, labels.shape[0], stride=SUB), :] = piece
        lane = lax.broadcasted_iota(jnp.int32, (SUB, LANES), 1)
        steps = []
        step = 1
        while step < MOSTSEG:
            steps.append(step)
            step *= 2
        for r in range(NRING):
            label = maps[r * SUB : (r + 1) * SUB, :]
            before = [(roll(label, d, 1) == label).astype(jnp.float32) for d in steps]
            after = [(roll(label, -d, 1) == label).astype(jnp.float32) for d in steps]

            def spread(x):
                total, rest = x, x
                for d, b, a in zip(steps, before, after):
                    total = total + b * roll(total, d, 1)
                    rest = rest + a * roll(rest, -d, 1)
                return total + rest - x

            inverse = 1.0 / spread(jnp.ones((SUB, LANES), jnp.float32))
            for c in range(3):
                for z in range(Z):
                    mean = spread(ext[c, r + 1, z + 2]) * inverse
                    low = roll(roll(mean, -wide, 1), 1, 0)
                    high = roll(roll(mean, wide, 1), -1, 0)
                    mean = jnp.where(lane < pad, low, mean)
                    mean = jnp.where(lane >= pad + wide, high, mean)
                    ext[c, r + 1, z + 2] = mean

    partners = n_ax - 1 + jnp.where(has_lo, n_ax, 0) + jnp.where(has_hi, n_ax, 0)
    pl.semaphore_wait(barrier, partners)

    rows, cols = pl.ds(1, R), pl.ds(2, Z)

    def halo(slot, src, dst, to_ax, to_rad):
        return pltpu.make_async_remote_copy(
            src_ref=ext.at[src], dst_ref=ext.at[dst], send_sem=halo_send.at[slot],
            recv_sem=halo_recv.at[slot], device_id=(to_ax, to_rad), device_id_type=MESH)

    everything = slice(None)
    z_lo = halo(0, (everything, rows, pl.ds(Z, 2)), (everything, rows, pl.ds(0, 2)), right, rad)
    z_hi = halo(1, (everything, rows, pl.ds(2, 2)), (everything, rows, pl.ds(Z + 2, 2)), left, rad)
    out_going = [
        halo(2, (everything, R, cols), (everything, 0, cols), ax, rad + 1),
        halo(3, (everything, R, Z + 1), (everything, 0, 1), right, rad + 1),
        halo(4, (everything, R, 2), (everything, 0, Z + 2), left, rad + 1),
    ]
    in_going = [
        halo(5, (everything, 1, cols), (everything, R + 1, cols), ax, rad - 1),
        halo(6, (everything, 1, Z + 1), (everything, R + 1, 1), right, rad - 1),
        halo(7, (everything, 1, 2), (everything, R + 1, Z + 2), left, rad - 1),
    ]

    z_lo.start()
    z_hi.start()

    def start_all(copies):
        for copy in copies:
            copy.start()

    def wait_recv(copies):
        for copy in copies:
            copy.wait_recv()

    def wait_send(copies):
        for copy in copies:
            copy.wait_send()

    pl.when(has_hi)(lambda: start_all(out_going))
    pl.when(has_lo)(lambda: start_all(in_going))
    wait_recv([z_lo, z_hi])
    pl.when(has_lo)(lambda: wait_recv(out_going))
    pl.when(has_hi)(lambda: wait_recv(in_going))

    @pl.when(rad == 0)
    def _():
        for c in range(3):
            for z in range(1, Z + 3):
                ext[c, 0, z] = SIGNS[c] * roll(ext[c, 1, z], half, 0)

    @pl.when(rad == n_rad - 1)
    def _():
        for c in range(3):
            for z in range(1, Z + 3):
                ext[c, R + 1, z] = jnp.zeros((SUB, LANES), jnp.float32)

    vel = [ext[c, 0 : R + 2, 1 : Z + 3] for c in range(3)]
    long = [ext[c, 1 : R + 1, 0 : Z + 4] for c in range(3)]
    grads = []
    for c in range(3):
        mid = vel[c][1:-1]
        grads.append([long[c][:, 2:] - long[c][:, :-2], vel[c][2:] - vel[c][:-2], up(mid) - down(mid)])
    tensor, mag = strain(grads)
    stress = [mag * t for t in tensor]
    w_own, w_lo, w_hi = [], [], []
    for c in range(3):
        w_own.append(smooth_t(smooth_z(long[c])))
        w_lo.append(smooth_t(smooth_z(vel[c][:1])))
        w_hi.append(smooth_t(smooth_z(vel[c][-1:])))
    w_grads = []
    for c in range(3):
        mid = w_own[c][:, 1:-1]
        column = jnp.concatenate([w_lo[c], mid, w_hi[c]], axis=0)
        w_grads.append([w_own[c][:, 2:] - w_own[c][:, :-2], column[2:] - column[:-2], up(mid) - down(mid)])
    w_tensor, w_mag = strain(w_grads)
    w_mag4 = 4.0 * w_mag
    lm, mm = 0.0, 0.0
    for number, (c, a) in enumerate(PAIRS):
        product = smooth_t(smooth_z(vel[c][1:-1] * vel[a][1:-1]))
        leonard = product - w_own[c][:, 1:-1] * w_own[a][:, 1:-1]
        model = smooth_t(smooth_z(stress[number])) - w_mag4 * w_tensor[number]
        lm = lm + PAIR_WEIGHTS[number] * leonard * model
        mm = mm + PAIR_WEIGHTS[number] * model * model
    sub_index = lax.broadcasted_iota(jnp.int32, (SUB, LANES), 0)
    lane_index = lax.broadcasted_iota(jnp.int32, (SUB, LANES), 1)
    mine = jnp.zeros((SUB, LANES), jnp.float32)
    for r in range(R):
        for base, quantity in ((0, lm), (half, mm)):
            row = jnp.sum(jnp.sum(quantity[r], axis=0), axis=0, keepdims=True)
            mine = jnp.where(sub_index == base + r, row, mine)
    mine = jnp.where((lane_index >= pad) & (lane_index < pad + wide), mine, 0.0)
    part[...] = mine

    def sums(side, i):
        peer = lax.rem(ax + i, n_ax)
        return pltpu.make_async_remote_copy(
            src_ref=part, dst_ref=parts.at[(1 - side) * n_ax + ax],
            send_sem=p_send.at[(1 + side) * n_ax + i], recv_sem=p_recv.at[(1 - side) * n_ax + ax],
            device_id=(peer, rad + side), device_id_type=MESH)

    def sums_in(side, i):
        peer = lax.rem(ax + i, n_ax)
        slot = (1 + side) * n_ax + peer
        return pltpu.make_async_remote_copy(
            src_ref=part, dst_ref=parts.at[slot],
            send_sem=p_send.at[(1 + side) * n_ax + i], recv_sem=p_recv.at[slot],
            device_id=(peer, rad + side), device_id_type=MESH)

    def first_of(side):
        return 1 if side == 0 else 0

    def send_sums(side):
        first = first_of(side)
        each(n_ax - first, lambda i: sums(side, i + first).start())

    send_sums(0)
    pl.when(has_lo)(lambda: send_sums(-1))
    pl.when(has_hi)(lambda: send_sums(1))

    for c in range(3):
        hx[c, 1 : R + 1] = stress[pair(c, 1)][:, 1:-1]

    def edge(slot, src, dst, to_rad):
        return pltpu.make_async_remote_copy(
            src_ref=hx.at[:, src], dst_ref=hx.at[:, dst], send_sem=h_send.at[slot],
            recv_sem=h_recv.at[slot], device_id=(ax, to_rad), device_id_type=MESH)

    edge_out = edge(0, R, 0, rad + 1)
    edge_in = edge(1, 1, R + 1, rad - 1)
    pl.when(has_hi)(lambda: edge_out.start())
    pl.when(has_lo)(lambda: edge_in.start())

    @pl.when(rad == 0)
    def _():
        for c in range(3):
            for z in range(Z):
                hx[c, 0, z] = SIGNS[c] * SIGNS[1] * roll(hx[c, 1, z], half, 0)

    @pl.when(rad == n_rad - 1)
    def _():
        for c in range(3):
            for z in range(Z):
                hx[c, R + 1, z] = jnp.zeros((SUB, LANES), jnp.float32)

    bases, turns = [], []
    for c in range(3):
        axial = vel[c][1:-1] * vel[0][1:-1]
        radial = vel[c][:, 1:-1] * vel[1][:, 1:-1]
        around = vel[c][1:-1, 1:-1] * vel[2][1:-1, 1:-1]
        change = axial[:, 2:] - axial[:, :-2] + (radial[2:] - radial[:-2]) + (up(around) - down(around))
        bases.append(vel[c][1:-1, 1:-1] - 0.5 * change)
        along = stress[pair(c, 0)]
        turn = stress[pair(c, 2)][:, 1:-1]
        turns.append(along[:, 2:] - along[:, :-2] + (up(turn) - down(turn)))

    count = n_ax * Z * T
    each(n_ax - 1, lambda i: sums_in(0, i + 1).wait_recv())

    def coefficients(total):
        total = jnp.broadcast_to(jnp.sum(total, axis=1, keepdims=True), (SUB, LANES)) / count
        return total / (roll(total, -half, 0) + EPSILON)

    def total_of(side):
        first = first_of(side)
        total = part[...] if first else jnp.zeros((SUB, LANES), jnp.float32)
        if n_ax <= 16:
            for i in range(first, n_ax):
                total = total + parts[(1 + side) * n_ax + lax.rem(ax + i, n_ax)]
            return total
        return lax.fori_loop(
            first, n_ax, lambda i, t: t + parts[(1 + side) * n_ax + lax.rem(ax + i, n_ax)], total)

    coef = coefficients(total_of(0))

    def beside(side, row):
        each(n_ax, lambda i: sums_in(side, i).wait_recv())
        edge_coef[0 if side < 0 else 1] = jnp.broadcast_to(
            coefficients(total_of(side))[row : row + 1], (SUB, LANES))

    pl.when(has_lo)(lambda: beside(-1, R - 1))
    pl.when(has_hi)(lambda: beside(1, 0))

    @pl.when(rad == 0)
    def _():
        edge_coef[0] = jnp.broadcast_to(coef[0:1], (SUB, LANES))

    @pl.when(rad == n_rad - 1)
    def _():
        edge_coef[1] = jnp.zeros((SUB, LANES), jnp.float32)

    pl.when(has_lo)(lambda: edge_out.wait_recv())
    pl.when(has_hi)(lambda: edge_in.wait_recv())
    by_row = [edge_coef[0]] + [jnp.broadcast_to(coef[r : r + 1], (SUB, LANES)) for r in range(R)] + [edge_coef[1]]
    for c in range(3):
        for r in range(R):
            new = bases[c][r] + by_row[r + 1] * turns[c][r]
            new = new + (by_row[r + 2] * hx[c, r + 2] - by_row[r] * hx[c, r])
            for z in range(Z):
                row = ((c * R + r) * Z + z) * SUB
                own[row : row + SUB, :] = new[z]
    for c in range(3):
        for r in range(R):
            pieces = [own[pl.ds((c * R + r) * Z * SUB + s, Z, stride=SUB), :] for s in range(SUB)]
            for k, tile in enumerate(joined(pieces, wide, pad)):
                out_ref[c, r, :, k * LANES : (k + 1) * LANES] = tile

    wait_send([z_lo, z_hi])

    @pl.when(has_hi)
    def _():
        wait_send(out_going + [edge_out])
        each(n_ax, lambda i: sums(1, i).wait_send())

    @pl.when(has_lo)
    def _():
        wait_send(in_going + [edge_in])
        each(n_ax, lambda i: sums(-1, i).wait_send())

    each(n_ax - 1, lambda i: sums(0, i + 1).wait_send())


def shards(n_ax, n_rad, velocity, cycle_map):
    _, R, Z, T = velocity.shape
    return pl.pallas_call(
        functools.partial(kernel, n_ax, n_rad),
        out_shape=jax.ShapeDtypeStruct(velocity.shape, velocity.dtype),
        in_specs=[pl.BlockSpec(memory_space=pltpu.VMEM)] * 2,
        out_specs=pl.BlockSpec(memory_space=pltpu.VMEM),
        scratch_shapes=[
            pltpu.VMEM((3 * R * Z * SUB, LANES), jnp.float32),
            pltpu.VMEM((NRING * SUB, LANES), jnp.float32),
            pltpu.VMEM((3, R + 2, Z + 4, SUB, LANES), jnp.float32),
            pltpu.VMEM((3, R + 2, Z, SUB, LANES), jnp.float32),
            pltpu.VMEM((SUB, LANES), jnp.float32),
            pltpu.VMEM((3 * n_ax, SUB, LANES), jnp.float32),
            pltpu.VMEM((2, SUB, LANES), jnp.float32),
            pltpu.SemaphoreType.DMA((8,)),
            pltpu.SemaphoreType.DMA((8,)),
            pltpu.SemaphoreType.DMA((2,)),
            pltpu.SemaphoreType.DMA((2,)),
            pltpu.SemaphoreType.DMA((3 * n_ax,)),
            pltpu.SemaphoreType.DMA((3 * n_ax,)),
        ],
        compiler_params=pltpu.CompilerParams(collective_id=0, has_side_effects=True),
    )(velocity, cycle_map)


def solution(mesh):
    n_ax, n_rad = mesh.shape["ax"], mesh.shape["rad"]
    spec = P(None, "rad", "ax", None)
    body = functools.partial(shards, n_ax, n_rad)
    return jax.shard_map(body, mesh=mesh, in_specs=(spec, P()), out_specs=spec, check_vma=False)
```

time: 57.2 us -> 21 us (0.37)
  starting transfers between devices: 21 us -> 0 us
  Pallas kernels: 0 us -> 19.3 us
  blocking collectives: 18.1 us -> 0 us
  waiting for transfers between devices: 8.3 us -> 0 us
  other arithmetic: 4.18 us -> 0 us
  local copies, waits for them, and re-layouts: 4.89 us -> 1.56 us
    ppermute x8 -> x0, starting transfers between devices: 21 us -> none  [the longest x4 11.7 us: with_halo(): lax.ppermute(tail, axis, [(i, (i + 1) % count) for i in range(ends)])]
    pallas_call x0 -> x1, Pallas kernels: none -> 19.3 us  [shards(): pl.pallas_call(functools.partial(kernel, n_ax, n_rad), out_shape=jax.Shap...]
    psum x1 -> x0, blocking collectives: 18.1 us -> none  [shards(): lm_total, mm_total = lax.psum((lm_rows, mm_rows), 'ax')]
    ppermute x8 -> x0, waiting for transfers between devices: 8.3 us -> none  [the longest x4 4.68 us: with_halo(): lax.ppermute(head, axis, [((i + 1) % count, i) for i in range(ends)])]
    slice x52 -> x0, local copies, waits for them, and re-layouts: 3.92 us -> none  [the longest x24 1.92 us: test_filter(): jnp.roll(along_axis, 1, 2) + 2.0 * along_axis + jnp.roll(along_axis, -1, 2)]
    mul x19 -> x0, other arithmetic: 1.64 us -> none  [the longest x11 0.46 us: test_filter(): (quantity[1:-1, :-2] + 2.0 * quantity[1:-1, 1:-1] + quantity[1:-1, 2:]) *...]
    another operation x5 -> x0, other arithmetic: 1.01 us -> none  [the longest x3 0.9 us: shards(): return jnp.stack(updated)]
    reduce_sum x2 -> x0, other arithmetic: 0.97 us -> none  [the longest x1 0.83 us: shards(): lm_rows = jnp.sum(leonard_model, axis=(1, 2))]
  transfers between devices with their start and end apart: 8 -> 0, of which waited for: 4 -> 0; matrix products, arithmetic and copies ran while one was open for 0% -> 0% of each run, Pallas kernels for 0% -> 0%
where the time goes in v1:
time: 21 us; the launch traced here: 20.9 us
  Pallas kernels  19.3 us (92%)
  local copies, waits for them, and re-layouts  1.56 us (7%)
    pallas_call x1, Pallas kernels, shards(): pl.pallas_call(functools.partial(kernel, n_ax, n_rad), out_shape=jax.Shap...  19.3 us
    unnamed x1, local copies, waits for them, and re-layouts  1.56 us

profile of v1, /device:TPU:1, one launch (start us, length us, event | category | flops | bytes accessed | tf_op | source)
XLA Modules:
  0.0 20.9 jit_solution(7899501739855991877)
XLA Ops:
  0.0 19.3 %shard_map.28 = f32[3,3,3,768]{3,2,1,0:T(4,128)} custom-call(f32[3,3,3,768]{3,2,1,0:T(4,128)} %v_ref.1, s32[3,768]{1,0:T(4,128)} %map_ref.1), custom_call_target="tpu_custom_call" | custom-call | tf_op jit(solution)/shard_map/pallas_call | solution.py:402
  19.3 1.6 %copy.4 = f32[3,3,3,768]{3,2,1,0:T(4,128)} copy(f32[3,3,3,768]{3,2,1,0:T(4,128)} %shard_map.28) | data formatting | bytes 165888

commit v2 on v1

--- a/solution.py
+++ b/solution.py
@@ -51,18 +51,22 @@
     return (x[:, :-2] + 2.0 * x[:, 1:-1] + x[:, 2:]) * 0.25
 
 
+def tiles_of(x):
+    return [x[:, k : k + LANES] for k in range(0, x.shape[1], LANES)]
+
+
 def segments(x, wide, pad):
-    rows, total = x.shape
-    tiles = total // LANES
+    rows, tiles = x[0].shape[0], len(x)
+    total = tiles * LANES
     lane = lax.broadcasted_iota(jnp.int32, (rows, LANES), 1)
     pieces = []
     for s in range(SUB):
         start = (s * wide - pad) % total
         k, off = start // LANES, start % LANES
-        first = x[:, k * LANES : (k + 1) * LANES]
+        first = x[k]
         if off:
             k2 = (k + 1) % tiles
-            second = x[:, k2 * LANES : (k2 + 1) * LANES]
+            second = x[k2]
             first = jnp.where(lane < LANES - off, roll(first, -off, 1), roll(second, -off, 1))
         pieces.append(first)
     return pieces
@@ -109,17 +113,20 @@
     return out
 
 
-def kernel(n_ax, n_rad, v_ref, map_ref, out_ref, own, maps, ext, hx, part, parts, edge_coef,
-           halo_send, halo_recv, h_send, h_recv, p_send, p_recv):
+def kernel(n_ax, n_rad, v_hbm, map_hbm, out_ref, nat, map_ref, own, maps, ext, hx, part, parts, edge_coef,
+           z_out, z_in, z_seg, in_sems, halo_send, halo_recv, h_send, h_recv, p_send, p_recv):
     rad = lax.axis_index("rad")
     ax = lax.axis_index("ax")
-    R, Z, T = v_ref.shape[1], v_ref.shape[2], v_ref.shape[3]
+    R, Z, T = nat.shape[1], nat.shape[2], nat.shape[3]
     wide = T // SUB
     pad = (LANES - wide) // 2
     half = SUB // 2
     right, left = lax.rem(ax + 1, n_ax), lax.rem(ax + n_ax - 1, n_ax)
     has_lo, has_hi = rad > 0, rad < n_rad - 1
 
+    def strips(c, r):
+        return [own[pl.ds((c * R + r) * Z * SUB + s, Z, stride=SUB), :] for s in range(SUB)]
+
     barrier = pltpu.get_barrier_semaphore()
 
     def greet(to_rad, first):
@@ -132,9 +139,15 @@
     pl.when(has_lo)(lambda: greet(rad - 1, 0))
     pl.when(has_hi)(lambda: greet(rad + 1, 0))
 
+    fetch = pltpu.make_async_copy(v_hbm, nat, in_sems.at[0])
+    fetch.start()
+    fetch_map = pltpu.make_async_copy(map_hbm, map_ref, in_sems.at[1])
+    fetch_map.start()
+    fetch.wait()
+    fetch_map.wait()
     for c in range(3):
         for r in range(R):
-            for s, piece in enumerate(segments(v_ref[c, r], wide, pad)):
+            for s, piece in enumerate(segments(tiles_of(nat[c, r]), wide, pad)):
                 own[pl.ds((c * R + r) * Z * SUB + s, Z, stride=SUB), :] = piece
     for c in range(3):
         for r in range(R):
@@ -145,7 +158,7 @@
     @pl.when(rad == 0)
     def _():
         labels = map_ref[...].astype(jnp.float32)
-        for s, piece in enumerate(segments(labels, wide, pad)):
+        for s, piece in enumerate(segments(tiles_of(labels), wide, pad)):
             maps[pl.ds(s, labels.shape[0], stride=SUB), :] = piece
         lane = lax.broadcasted_iota(jnp.int32, (SUB, LANES), 1)
         steps = []
@@ -174,6 +187,20 @@
                     mean = jnp.where(lane < pad, low, mean)
                     mean = jnp.where(lane >= pad + wide, high, mean)
                     ext[c, r + 1, z + 2] = mean
+                    row = ((c * R + r) * Z + z) * SUB
+                    own[row : row + SUB, :] = mean
+        for c in range(3):
+            for r in range(NRING):
+                for k, tile in enumerate(joined(strips(c, r), wide, pad)):
+                    nat[c, r, :, k * LANES : (k + 1) * LANES] = tile
+
+    n_rows = 3 * R * 2
+    for side, first in ((0, Z - 2), (1, 0)):
+        for c in range(3):
+            for r in range(R):
+                for k in range(T // LANES):
+                    row = k * n_rows + (c * R + r) * 2
+                    z_out[side, row : row + 2, :] = nat[c, r, first : first + 2, k * LANES : (k + 1) * LANES]
 
     partners = n_ax - 1 + jnp.where(has_lo, n_ax, 0) + jnp.where(has_hi, n_ax, 0)
     pl.semaphore_wait(barrier, partners)
@@ -186,8 +213,13 @@
             recv_sem=halo_recv.at[slot], device_id=(to_ax, to_rad), device_id_type=MESH)
 
     everything = slice(None)
-    z_lo = halo(0, (everything, rows, pl.ds(Z, 2)), (everything, rows, pl.ds(0, 2)), right, rad)
-    z_hi = halo(1, (everything, rows, pl.ds(2, 2)), (everything, rows, pl.ds(Z + 2, 2)), left, rad)
+
+    def z_halo(slot, to_ax):
+        return pltpu.make_async_remote_copy(
+            src_ref=z_out.at[slot], dst_ref=z_in.at[slot], send_sem=halo_send.at[slot],
+            recv_sem=halo_recv.at[slot], device_id=(to_ax, rad), device_id_type=MESH)
+
+    z_lo, z_hi = z_halo(0, right), z_halo(1, left)
     out_going = [
         halo(2, (everything, R, cols), (everything, 0, cols), ax, rad + 1),
         halo(3, (everything, R, Z + 1), (everything, 0, 1), right, rad + 1),
@@ -216,7 +248,16 @@
 
     pl.when(has_hi)(lambda: start_all(out_going))
     pl.when(has_lo)(lambda: start_all(in_going))
-    wait_recv([z_lo, z_hi])
+    for side, copy, first in ((0, z_lo, 0), (1, z_hi, Z + 2)):
+        copy.wait_recv()
+        tiles = [z_in[side, k * n_rows : (k + 1) * n_rows, :] for k in range(T // LANES)]
+        for s, piece in enumerate(segments(tiles, wide, pad)):
+            z_seg[pl.ds(side * n_rows * SUB + s, n_rows, stride=SUB), :] = piece
+        for c in range(3):
+            for r in range(R):
+                for z in range(2):
+                    row = (side * n_rows + (c * R + r) * 2 + z) * SUB
+                    ext[c, r + 1, first + z] = z_seg[row : row + SUB, :]
     pl.when(has_lo)(lambda: wait_recv(out_going))
     pl.when(has_hi)(lambda: wait_recv(in_going))
 
@@ -267,7 +308,12 @@
             row = jnp.sum(jnp.sum(quantity[r], axis=0), axis=0, keepdims=True)
             mine = jnp.where(sub_index == base + r, row, mine)
     mine = jnp.where((lane_index >= pad) & (lane_index < pad + wide), mine, 0.0)
-    part[...] = mine
+    fold = LANES // 2
+    while fold >= LANES // SUB:
+        mine = mine + roll(mine, fold, 1)
+        fold //= 2
+    group = lane_index // (LANES // SUB) == sub_index
+    part[...] = jnp.sum(jnp.where(group, mine, 0.0), axis=0, keepdims=True)
 
     def sums(side, i):
         peer = lax.rem(ax + i, n_ax)
@@ -335,12 +381,12 @@
     each(n_ax - 1, lambda i: sums_in(0, i + 1).wait_recv())
 
     def coefficients(total):
-        total = jnp.broadcast_to(jnp.sum(total, axis=1, keepdims=True), (SUB, LANES)) / count
+        total = jnp.broadcast_to(jnp.sum(jnp.where(group, total, 0.0), axis=1, keepdims=True), (SUB, LANES)) / count
         return total / (roll(total, -half, 0) + EPSILON)
 
     def total_of(side):
         first = first_of(side)
-        total = part[...] if first else jnp.zeros((SUB, LANES), jnp.float32)
+        total = part[...] if first else jnp.zeros((1, LANES), jnp.float32)
         if n_ax <= 16:
             for i in range(first, n_ax):
                 total = total + parts[(1 + side) * n_ax + lax.rem(ax + i, n_ax)]
@@ -378,8 +424,7 @@
                 own[row : row + SUB, :] = new[z]
     for c in range(3):
         for r in range(R):
-            pieces = [own[pl.ds((c * R + r) * Z * SUB + s, Z, stride=SUB), :] for s in range(SUB)]
-            for k, tile in enumerate(joined(pieces, wide, pad)):
+            for k, tile in enumerate(joined(strips(c, r), wide, pad)):
                 out_ref[c, r, :, k * LANES : (k + 1) * LANES] = tile
 
     wait_send([z_lo, z_hi])
@@ -402,16 +447,22 @@
     return pl.pallas_call(
         functools.partial(kernel, n_ax, n_rad),
         out_shape=jax.ShapeDtypeStruct(velocity.shape, velocity.dtype),
-        in_specs=[pl.BlockSpec(memory_space=pltpu.VMEM)] * 2,
+        in_specs=[pl.BlockSpec(memory_space=pltpu.HBM)] * 2,
         out_specs=pl.BlockSpec(memory_space=pltpu.VMEM),
         scratch_shapes=[
+            pltpu.VMEM(velocity.shape, jnp.float32),
+            pltpu.VMEM(cycle_map.shape, jnp.int32),
             pltpu.VMEM((3 * R * Z * SUB, LANES), jnp.float32),
             pltpu.VMEM((NRING * SUB, LANES), jnp.float32),
             pltpu.VMEM((3, R + 2, Z + 4, SUB, LANES), jnp.float32),
             pltpu.VMEM((3, R + 2, Z, SUB, LANES), jnp.float32),
-            pltpu.VMEM((SUB, LANES), jnp.float32),
-            pltpu.VMEM((3 * n_ax, SUB, LANES), jnp.float32),
+            pltpu.VMEM((1, LANES), jnp.float32),
+            pltpu.VMEM((3 * n_ax, 1, LANES), jnp.float32),
             pltpu.VMEM((2, SUB, LANES), jnp.float32),
+            pltpu.VMEM((2, 3 * R * 2 * T // LANES, LANES), jnp.float32),
+            pltpu.VMEM((2, 3 * R * 2 * T // LANES, LANES), jnp.float32),
+            pltpu.VMEM((2 * 3 * R * 2 * SUB, LANES), jnp.float32),
+            pltpu.SemaphoreType.DMA((2,)),
             pltpu.SemaphoreType.DMA((8,)),
             pltpu.SemaphoreType.DMA((8,)),
             pltpu.SemaphoreType.DMA((2,)),
@@ -419,8 +470,8 @@
             pltpu.SemaphoreType.DMA((3 * n_ax,)),
             pltpu.SemaphoreType.DMA((3 * n_ax,)),
         ],
-        compiler_params=pltpu.CompilerParams(collective_id=0, has_side_effects=True),
-    )(velocity, cycle_map)
+        compiler_params=pltpu.CompilerParams(collective_id=0, has_side_effects=True, vmem_limit_bytes=8 << 20),
+    )(*(pltpu.with_memory_space_constraint(x, pltpu.HBM) for x in (velocity, cycle_map)))
 
 
 def solution(mesh):

time: 21 us -> 18.1 us (0.86)
  Pallas kernels: 19.3 us -> 17.3 us
  local copies, waits for them, and re-layouts: 1.56 us -> 0.65 us
    pallas_call x1, Pallas kernels: 19.3 us -> 17.3 us  [shards(): pl.pallas_call(functools.partial(kernel, n_ax, n_rad), out_shape=jax.Shap...]
    unnamed x1, local copies, waits for them, and re-layouts: 1.56 us -> 0.65 us
where the time goes in v2:
time: 18.1 us; the launch traced here: 18 us
  Pallas kernels  17.3 us (96%)
  local copies, waits for them, and re-layouts  0.65 us (4%)
    pallas_call x1, Pallas kernels, shards(): pl.pallas_call(functools.partial(kernel, n_ax, n_rad), out_shape=jax.Shap...  17.3 us
    unnamed x1, local copies, waits for them, and re-layouts  0.65 us

profile of v2, /device:TPU:1, one launch (start us, length us, event | category | flops | bytes accessed | tf_op | source)
XLA Modules:
  0.0 18.0 jit_solution(1804737892484891887)
XLA Ops:
  0.0 17.3 %shard_map.28 = f32[3,3,3,768]{3,2,1,0:T(4,128)S(1)} custom-call(f32[3,3,3,768]{3,2,1,0:T(4,128)} %v_hbm.1, s32[3,768]{1,0:T(4,128)} %map_hbm.1), custom_call_target="tpu_custom_call" | custom-call | tf_op jit(solution)/shard_map/pallas_call | solution.py:447
  17.3 0.6 %copy.4 = f32[3,3,3,768]{3,2,1,0:T(4,128)} copy(f32[3,3,3,768]{3,2,1,0:T(4,128)S(1)} %shard_map.28) | data formatting | bytes 165888

commit v3 on v2

--- a/solution.py
+++ b/solution.py
@@ -113,8 +113,19 @@
     return out
 
 
+def stages(n_ax):
+    distances, own, beside = [1], 2, 1
+    while own < n_ax // 2:
+        distances.append(own)
+        own, beside = 2 * own, beside + own
+    while beside < n_ax // 2:
+        distances.append(1)
+        beside += 1
+    return distances
+
+
 def kernel(n_ax, n_rad, v_hbm, map_hbm, out_ref, nat, map_ref, own, maps, ext, hx, part, parts, edge_coef,
-           z_out, z_in, z_seg, in_sems, halo_send, halo_recv, h_send, h_recv, p_send, p_recv):
+           z_out, z_in, z_seg, ready, in_sems, halo_send, halo_recv, h_send, h_recv, p_send, p_recv):
     rad = lax.axis_index("rad")
     ax = lax.axis_index("ax")
     R, Z, T = nat.shape[1], nat.shape[2], nat.shape[3]
@@ -129,71 +140,29 @@
 
     barrier = pltpu.get_barrier_semaphore()
 
-    def greet(to_rad, first):
-        def body(i):
-            peer = lax.rem(ax + first + i, n_ax)
-            pl.semaphore_signal(barrier, inc=1, device_id=(peer, to_rad), device_id_type=MESH)
-        each(n_ax - first, body)
-
-    greet(rad, 1)
-    pl.when(has_lo)(lambda: greet(rad - 1, 0))
-    pl.when(has_hi)(lambda: greet(rad + 1, 0))
+    def greet(to_ax, to_rad):
+        pl.semaphore_signal(barrier, inc=1, device_id=(to_ax, to_rad), device_id_type=MESH)
+
+    greet(left, rad)
+    greet(right, rad)
+    pl.when(has_lo)(lambda: greet(ax, rad - 1))
+    pl.when(has_hi)(lambda: greet(ax, rad + 1))
+
+    distances = stages(n_ax)
+
+    def tell(stage):
+        d = distances[stage]
+        for peer in (lax.rem(ax + d, n_ax), lax.rem(ax + n_ax - d, n_ax)):
+            pl.semaphore_signal(ready.at[stage], inc=1, device_id=(peer, rad), device_id_type=MESH)
+
+    def hear(stage):
+        pl.semaphore_wait(ready.at[stage], 2)
 
     fetch = pltpu.make_async_copy(v_hbm, nat, in_sems.at[0])
     fetch.start()
     fetch_map = pltpu.make_async_copy(map_hbm, map_ref, in_sems.at[1])
-    fetch_map.start()
+    pl.when(rad == 0)(lambda: fetch_map.start())
     fetch.wait()
-    fetch_map.wait()
-    for c in range(3):
-        for r in range(R):
-            for s, piece in enumerate(segments(tiles_of(nat[c, r]), wide, pad)):
-                own[pl.ds((c * R + r) * Z * SUB + s, Z, stride=SUB), :] = piece
-    for c in range(3):
-        for r in range(R):
-            for z in range(Z):
-                row = ((c * R + r) * Z + z) * SUB
-                ext[c, r + 1, z + 2] = own[row : row + SUB, :]
-
-    @pl.when(rad == 0)
-    def _():
-        labels = map_ref[...].astype(jnp.float32)
-        for s, piece in enumerate(segments(tiles_of(labels), wide, pad)):
-            maps[pl.ds(s, labels.shape[0], stride=SUB), :] = piece
-        lane = lax.broadcasted_iota(jnp.int32, (SUB, LANES), 1)
-        steps = []
-        step = 1
-        while step < MOSTSEG:
-            steps.append(step)
-            step *= 2
-        for r in range(NRING):
-            label = maps[r * SUB : (r + 1) * SUB, :]
-            before = [(roll(label, d, 1) == label).astype(jnp.float32) for d in steps]
-            after = [(roll(label, -d, 1) == label).astype(jnp.float32) for d in steps]
-
-            def spread(x):
-                total, rest = x, x
-                for d, b, a in zip(steps, before, after):
-                    total = total + b * roll(total, d, 1)
-                    rest = rest + a * roll(rest, -d, 1)
-                return total + rest - x
-
-            inverse = 1.0 / spread(jnp.ones((SUB, LANES), jnp.float32))
-            for c in range(3):
-                for z in range(Z):
-                    mean = spread(ext[c, r + 1, z + 2]) * inverse
-                    low = roll(roll(mean, -wide, 1), 1, 0)
-                    high = roll(roll(mean, wide, 1), -1, 0)
-                    mean = jnp.where(lane < pad, low, mean)
-                    mean = jnp.where(lane >= pad + wide, high, mean)
-                    ext[c, r + 1, z + 2] = mean
-                    row = ((c * R + r) * Z + z) * SUB
-                    own[row : row + SUB, :] = mean
-        for c in range(3):
-            for r in range(NRING):
-                for k, tile in enumerate(joined(strips(c, r), wide, pad)):
-                    nat[c, r, :, k * LANES : (k + 1) * LANES] = tile
-
     n_rows = 3 * R * 2
     for side, first in ((0, Z - 2), (1, 0)):
         for c in range(3):
@@ -202,8 +171,66 @@
                     row = k * n_rows + (c * R + r) * 2
                     z_out[side, row : row + 2, :] = nat[c, r, first : first + 2, k * LANES : (k + 1) * LANES]
 
-    partners = n_ax - 1 + jnp.where(has_lo, n_ax, 0) + jnp.where(has_hi, n_ax, 0)
-    pl.semaphore_wait(barrier, partners)
+    pl.semaphore_wait(barrier, 2 + jnp.where(has_lo, 1, 0) + jnp.where(has_hi, 1, 0))
+
+    def z_halo(slot, to_ax):
+        return pltpu.make_async_remote_copy(
+            src_ref=z_out.at[slot], dst_ref=z_in.at[slot], send_sem=halo_send.at[slot],
+            recv_sem=halo_recv.at[slot], device_id=(to_ax, rad), device_id_type=MESH)
+
+    z_lo, z_hi = z_halo(0, right), z_halo(1, left)
+    z_lo.start()
+    z_hi.start()
+    tell(0)
+
+    for c in range(3):
+        for r in range(R):
+            for s, piece in enumerate(segments(tiles_of(nat[c, r]), wide, pad)):
+                own[pl.ds((c * R + r) * Z * SUB + s, Z, stride=SUB), :] = piece
+    for c in range(3):
+        for r in range(R):
+            for z in range(Z):
+                row = ((c * R + r) * Z + z) * SUB
+                ext[c, r + 1, z + 2] = own[row : row + SUB, :]
+
+    lane = lax.broadcasted_iota(jnp.int32, (SUB, LANES), 1)
+    steps = []
+    while 2 ** len(steps) < MOSTSEG:
+        steps.append(2 ** len(steps))
+
+    def cell_sums(r):
+        label = maps[r * SUB : (r + 1) * SUB, :]
+        before = [(roll(label, d, 1) == label).astype(jnp.float32) for d in steps]
+        after = [(roll(label, -d, 1) == label).astype(jnp.float32) for d in steps]
+
+        def spread(x):
+            total, rest = x, x
+            for d, b, a in zip(steps, before, after):
+                total = total + b * roll(total, d, 1)
+                rest = rest + a * roll(rest, -d, 1)
+            return total + rest - x
+
+        return spread
+
+    def coarsen(r, spread, c, z):
+        mean = spread(ext[c, r + 1, z]) * maps[(NRING + r) * SUB : (NRING + r + 1) * SUB, :]
+        low = roll(roll(mean, -wide, 1), 1, 0)
+        high = roll(roll(mean, wide, 1), -1, 0)
+        mean = jnp.where(lane < pad, low, mean)
+        ext[c, r + 1, z] = jnp.where(lane >= pad + wide, high, mean)
+
+    @pl.when(rad == 0)
+    def _():
+        fetch_map.wait()
+        labels = map_ref[...].astype(jnp.float32)
+        for s, piece in enumerate(segments(tiles_of(labels), wide, pad)):
+            maps[pl.ds(s, NRING, stride=SUB), :] = piece
+        for r in range(NRING):
+            spread = cell_sums(r)
+            maps[(NRING + r) * SUB : (NRING + r + 1) * SUB, :] = 1.0 / spread(jnp.ones((SUB, LANES), jnp.float32))
+            for c in range(3):
+                for z in range(Z):
+                    coarsen(r, spread, c, z + 2)
 
     rows, cols = pl.ds(1, R), pl.ds(2, Z)
 
@@ -214,12 +241,6 @@
 
     everything = slice(None)
 
-    def z_halo(slot, to_ax):
-        return pltpu.make_async_remote_copy(
-            src_ref=z_out.at[slot], dst_ref=z_in.at[slot], send_sem=halo_send.at[slot],
-            recv_sem=halo_recv.at[slot], device_id=(to_ax, rad), device_id_type=MESH)
-
-    z_lo, z_hi = z_halo(0, right), z_halo(1, left)
     out_going = [
         halo(2, (everything, R, cols), (everything, 0, cols), ax, rad + 1),
         halo(3, (everything, R, Z + 1), (everything, 0, 1), right, rad + 1),
@@ -231,9 +252,6 @@
         halo(7, (everything, 1, 2), (everything, R + 1, Z + 2), left, rad - 1),
     ]
 
-    z_lo.start()
-    z_hi.start()
-
     def start_all(copies):
         for copy in copies:
             copy.start()
@@ -246,8 +264,13 @@
         for copy in copies:
             copy.wait_send()
 
-    pl.when(has_hi)(lambda: start_all(out_going))
-    pl.when(has_lo)(lambda: start_all(in_going))
+    pl.when(has_hi)(lambda: start_all(out_going[:1]))
+    pl.when(has_lo)(lambda: start_all(in_going[:1]))
+    for stage in range(len(distances) - 1)[:1]:
+        hear(stage)
+        tell(stage + 1)
+    pl.when(has_hi)(lambda: start_all(out_going[1:]))
+    pl.when(has_lo)(lambda: start_all(in_going[1:]))
     for side, copy, first in ((0, z_lo, 0), (1, z_hi, Z + 2)):
         copy.wait_recv()
         tiles = [z_in[side, k * n_rows : (k + 1) * n_rows, :] for k in range(T // LANES)]
@@ -258,6 +281,31 @@
                 for z in range(2):
                     row = (side * n_rows + (c * R + r) * 2 + z) * SUB
                     ext[c, r + 1, first + z] = z_seg[row : row + SUB, :]
+    @pl.when(rad == 0)
+    def _():
+        for r in range(NRING):
+            spread = cell_sums(r)
+            for c in range(3):
+                for z in (0, 1, Z + 2, Z + 3):
+                    coarsen(r, spread, c, z)
+
+    for stage in range(1, len(distances) - 1):
+        hear(stage)
+        tell(stage + 1)
+
+    long = [ext[c, 1 : R + 1, 0 : Z + 4] for c in range(3)]
+    mids = [x[:, 1:-1] for x in long]
+    grads, w_own, w_grads, leonards = [], [], [], []
+    for c in range(3):
+        turned = up(mids[c]) - down(mids[c])
+        grads.append([long[c][:, 2:] - long[c][:, :-2], None, turned])
+        w_own.append(smooth_t(smooth_z(long[c])))
+        mid = w_own[c][:, 1:-1]
+        w_grads.append([w_own[c][:, 2:] - w_own[c][:, :-2], None, up(mid) - down(mid)])
+    for c, a in PAIRS:
+        product = smooth_t(smooth_z(mids[c] * mids[a]))
+        leonards.append(product - w_own[c][:, 1:-1] * w_own[a][:, 1:-1])
+
     pl.when(has_lo)(lambda: wait_recv(out_going))
     pl.when(has_hi)(lambda: wait_recv(in_going))
 
@@ -273,30 +321,20 @@
             for z in range(1, Z + 3):
                 ext[c, R + 1, z] = jnp.zeros((SUB, LANES), jnp.float32)
 
-    vel = [ext[c, 0 : R + 2, 1 : Z + 3] for c in range(3)]
-    long = [ext[c, 1 : R + 1, 0 : Z + 4] for c in range(3)]
-    grads = []
-    for c in range(3):
-        mid = vel[c][1:-1]
-        grads.append([long[c][:, 2:] - long[c][:, :-2], vel[c][2:] - vel[c][:-2], up(mid) - down(mid)])
+    below = [ext[c, 0:1, 1 : Z + 3] for c in range(3)]
+    above = [ext[c, R + 1 : R + 2, 1 : Z + 3] for c in range(3)]
+    for c in range(3):
+        column = jnp.concatenate([below[c], mids[c], above[c]], axis=0)
+        grads[c][1] = column[2:] - column[:-2]
+        column = jnp.concatenate(
+            [smooth_t(smooth_z(below[c])), w_own[c][:, 1:-1], smooth_t(smooth_z(above[c]))], axis=0)
+        w_grads[c][1] = column[2:] - column[:-2]
     tensor, mag = strain(grads)
     stress = [mag * t for t in tensor]
-    w_own, w_lo, w_hi = [], [], []
-    for c in range(3):
-        w_own.append(smooth_t(smooth_z(long[c])))
-        w_lo.append(smooth_t(smooth_z(vel[c][:1])))
-        w_hi.append(smooth_t(smooth_z(vel[c][-1:])))
-    w_grads = []
-    for c in range(3):
-        mid = w_own[c][:, 1:-1]
-        column = jnp.concatenate([w_lo[c], mid, w_hi[c]], axis=0)
-        w_grads.append([w_own[c][:, 2:] - w_own[c][:, :-2], column[2:] - column[:-2], up(mid) - down(mid)])
     w_tensor, w_mag = strain(w_grads)
     w_mag4 = 4.0 * w_mag
     lm, mm = 0.0, 0.0
-    for number, (c, a) in enumerate(PAIRS):
-        product = smooth_t(smooth_z(vel[c][1:-1] * vel[a][1:-1]))
-        leonard = product - w_own[c][:, 1:-1] * w_own[a][:, 1:-1]
+    for number, leonard in enumerate(leonards):
         model = smooth_t(smooth_z(stress[number])) - w_mag4 * w_tensor[number]
         lm = lm + PAIR_WEIGHTS[number] * leonard * model
         mm = mm + PAIR_WEIGHTS[number] * model * model
@@ -338,6 +376,7 @@
         each(n_ax - first, lambda i: sums(side, i + first).start())
 
     send_sums(0)
+    hear(len(distances) - 1)
     pl.when(has_lo)(lambda: send_sums(-1))
     pl.when(has_hi)(lambda: send_sums(1))
 
@@ -367,12 +406,13 @@
                 hx[c, R + 1, z] = jnp.zeros((SUB, LANES), jnp.float32)
 
     bases, turns = [], []
-    for c in range(3):
-        axial = vel[c][1:-1] * vel[0][1:-1]
-        radial = vel[c][:, 1:-1] * vel[1][:, 1:-1]
-        around = vel[c][1:-1, 1:-1] * vel[2][1:-1, 1:-1]
+    whole = [jnp.concatenate([below[c], mids[c], above[c]], axis=0)[:, 1:-1] for c in range(3)]
+    for c in range(3):
+        axial = mids[c] * mids[0]
+        radial = whole[c] * whole[1]
+        around = whole[c][1:-1] * whole[2][1:-1]
         change = axial[:, 2:] - axial[:, :-2] + (radial[2:] - radial[:-2]) + (up(around) - down(around))
-        bases.append(vel[c][1:-1, 1:-1] - 0.5 * change)
+        bases.append(whole[c][1:-1] - 0.5 * change)
         along = stress[pair(c, 0)]
         turn = stress[pair(c, 2)][:, 1:-1]
         turns.append(along[:, 2:] - along[:, :-2] + (up(turn) - down(turn)))
@@ -453,7 +493,7 @@
             pltpu.VMEM(velocity.shape, jnp.float32),
             pltpu.VMEM(cycle_map.shape, jnp.int32),
             pltpu.VMEM((3 * R * Z * SUB, LANES), jnp.float32),
-            pltpu.VMEM((NRING * SUB, LANES), jnp.float32),
+            pltpu.VMEM((2 * NRING * SUB, LANES), jnp.float32),
             pltpu.VMEM((3, R + 2, Z + 4, SUB, LANES), jnp.float32),
             pltpu.VMEM((3, R + 2, Z, SUB, LANES), jnp.float32),
             pltpu.VMEM((1, LANES), jnp.float32),
@@ -462,6 +502,7 @@
             pltpu.VMEM((2, 3 * R * 2 * T // LANES, LANES), jnp.float32),
             pltpu.VMEM((2, 3 * R * 2 * T // LANES, LANES), jnp.float32),
             pltpu.VMEM((2 * 3 * R * 2 * SUB, LANES), jnp.float32),
+            pltpu.SemaphoreType.REGULAR((len(stages(n_ax)),)),
             pltpu.SemaphoreType.DMA((2,)),
             pltpu.SemaphoreType.DMA((8,)),
             pltpu.SemaphoreType.DMA((8,)),

time: 18.1 us -> 18.6 us (1.028); the launches traced: 18 us -> 18.3 us
  Pallas kernels: 17.3 us -> 17.6 us
    pallas_call x1, Pallas kernels: 17.3 us -> 17.6 us  [shards(): pl.pallas_call(functools.partial(kernel, n_ax, n_rad), out_shape=jax.Shap...]
where the time goes in v3:
time: 18.6 us; the launch traced here: 18.3 us
  Pallas kernels  17.6 us (95%)
  local copies, waits for them, and re-layouts  0.65 us (3%)
    pallas_call x1, Pallas kernels, shards(): pl.pallas_call(functools.partial(kernel, n_ax, n_rad), out_shape=jax.Shap...  17.6 us
    unnamed x1, local copies, waits for them, and re-layouts  0.65 us

profile of v3, /device:TPU:1, one launch (start us, length us, event | category | flops | bytes accessed | tf_op | source)
XLA Modules:
  0.0 18.3 jit_solution(17931128213166165265)
XLA Ops:
  0.0 17.6 %shard_map.28 = f32[3,3,3,768]{3,2,1,0:T(4,128)S(1)} custom-call(f32[3,3,3,768]{3,2,1,0:T(4,128)} %v_hbm.1, s32[3,768]{1,0:T(4,128)} %map_hbm.1), custom_call_target="tpu_custom_call" | custom-call | tf_op jit(solution)/shard_map/pallas_call | solution.py:487
  17.6 0.6 %copy.4 = f32[3,3,3,768]{3,2,1,0:T(4,128)} copy(f32[3,3,3,768]{3,2,1,0:T(4,128)S(1)} %shard_map.28) | data formatting | bytes 165888

commit v4 on v3

--- a/solution.py
+++ b/solution.py
@@ -163,26 +163,6 @@
     fetch_map = pltpu.make_async_copy(map_hbm, map_ref, in_sems.at[1])
     pl.when(rad == 0)(lambda: fetch_map.start())
     fetch.wait()
-    n_rows = 3 * R * 2
-    for side, first in ((0, Z - 2), (1, 0)):
-        for c in range(3):
-            for r in range(R):
-                for k in range(T // LANES):
-                    row = k * n_rows + (c * R + r) * 2
-                    z_out[side, row : row + 2, :] = nat[c, r, first : first + 2, k * LANES : (k + 1) * LANES]
-
-    pl.semaphore_wait(barrier, 2 + jnp.where(has_lo, 1, 0) + jnp.where(has_hi, 1, 0))
-
-    def z_halo(slot, to_ax):
-        return pltpu.make_async_remote_copy(
-            src_ref=z_out.at[slot], dst_ref=z_in.at[slot], send_sem=halo_send.at[slot],
-            recv_sem=halo_recv.at[slot], device_id=(to_ax, rad), device_id_type=MESH)
-
-    z_lo, z_hi = z_halo(0, right), z_halo(1, left)
-    z_lo.start()
-    z_hi.start()
-    tell(0)
-
     for c in range(3):
         for r in range(R):
             for s, piece in enumerate(segments(tiles_of(nat[c, r]), wide, pad)):
@@ -231,6 +211,30 @@
             for c in range(3):
                 for z in range(Z):
                     coarsen(r, spread, c, z + 2)
+                    row = ((c * R + r) * Z + z) * SUB
+                    own[row : row + SUB, :] = ext[c, r + 1, z + 2]
+                for k, tile in enumerate(joined(strips(c, r), wide, pad)):
+                    nat[c, r, :, k * LANES : (k + 1) * LANES] = tile
+
+    n_rows = 3 * R * 2
+    for side, first in ((0, Z - 2), (1, 0)):
+        for c in range(3):
+            for r in range(R):
+                for k in range(T // LANES):
+                    row = k * n_rows + (c * R + r) * 2
+                    z_out[side, row : row + 2, :] = nat[c, r, first : first + 2, k * LANES : (k + 1) * LANES]
+
+    pl.semaphore_wait(barrier, 2 + jnp.where(has_lo, 1, 0) + jnp.where(has_hi, 1, 0))
+
+    def z_halo(slot, to_ax):
+        return pltpu.make_async_remote_copy(
+            src_ref=z_out.at[slot], dst_ref=z_in.at[slot], send_sem=halo_send.at[slot],
+            recv_sem=halo_recv.at[slot], device_id=(to_ax, rad), device_id_type=MESH)
+
+    z_lo, z_hi = z_halo(0, right), z_halo(1, left)
+    z_lo.start()
+    z_hi.start()
+    tell(0)
 
     rows, cols = pl.ds(1, R), pl.ds(2, Z)
 
@@ -281,14 +285,6 @@
                 for z in range(2):
                     row = (side * n_rows + (c * R + r) * 2 + z) * SUB
                     ext[c, r + 1, first + z] = z_seg[row : row + SUB, :]
-    @pl.when(rad == 0)
-    def _():
-        for r in range(NRING):
-            spread = cell_sums(r)
-            for c in range(3):
-                for z in (0, 1, Z + 2, Z + 3):
-                    coarsen(r, spread, c, z)
-
     for stage in range(1, len(distances) - 1):
         hear(stage)
         tell(stage + 1)

time: 18.6 us -> 17.9 us (0.962)
  Pallas kernels: 17.6 us -> 17.1 us
    pallas_call x1, Pallas kernels: 17.6 us -> 17.1 us  [shards(): pl.pallas_call(functools.partial(kernel, n_ax, n_rad), out_shape=jax.Shap...]
where the time goes in v4:
time: 17.9 us; the launch traced here: 17.8 us
  Pallas kernels  17.1 us (96%)
  local copies, waits for them, and re-layouts  0.65 us (4%)
    pallas_call x1, Pallas kernels, shards(): pl.pallas_call(functools.partial(kernel, n_ax, n_rad), out_shape=jax.Shap...  17.1 us
    unnamed x1, local copies, waits for them, and re-layouts  0.65 us

profile of v4, /device:TPU:1, one launch (start us, length us, event | category | flops | bytes accessed | tf_op | source)
XLA Modules:
  0.0 17.8 jit_solution(14196215932095643542)
XLA Ops:
  0.0 17.1 %shard_map.28 = f32[3,3,3,768]{3,2,1,0:T(4,128)S(1)} custom-call(f32[3,3,3,768]{3,2,1,0:T(4,128)} %v_hbm.1, s32[3,768]{1,0:T(4,128)} %map_hbm.1), custom_call_target="tpu_custom_call" | custom-call | tf_op jit(solution)/shard_map/pallas_call | solution.py:483
  17.1 0.6 %copy.4 = f32[3,3,3,768]{3,2,1,0:T(4,128)} copy(f32[3,3,3,768]{3,2,1,0:T(4,128)S(1)} %shard_map.28) | data formatting | bytes 165888

commit v5 on v4

--- a/solution.py
+++ b/solution.py
@@ -247,13 +247,13 @@
 
     out_going = [
         halo(2, (everything, R, cols), (everything, 0, cols), ax, rad + 1),
-        halo(3, (everything, R, Z + 1), (everything, 0, 1), right, rad + 1),
-        halo(4, (everything, R, 2), (everything, 0, Z + 2), left, rad + 1),
+        halo(3, (everything, R, 1), (everything, 0, 1), ax, rad + 1),
+        halo(4, (everything, R, Z + 2), (everything, 0, Z + 2), ax, rad + 1),
     ]
     in_going = [
         halo(5, (everything, 1, cols), (everything, R + 1, cols), ax, rad - 1),
-        halo(6, (everything, 1, Z + 1), (everything, R + 1, 1), right, rad - 1),
-        halo(7, (everything, 1, 2), (everything, R + 1, Z + 2), left, rad - 1),
+        halo(6, (everything, 1, 1), (everything, R + 1, 1), ax, rad - 1),
+        halo(7, (everything, 1, Z + 2), (everything, R + 1, Z + 2), ax, rad - 1),
     ]
 
     def start_all(copies):
@@ -273,8 +273,6 @@
     for stage in range(len(distances) - 1)[:1]:
         hear(stage)
         tell(stage + 1)
-    pl.when(has_hi)(lambda: start_all(out_going[1:]))
-    pl.when(has_lo)(lambda: start_all(in_going[1:]))
     for side, copy, first in ((0, z_lo, 0), (1, z_hi, Z + 2)):
         copy.wait_recv()
         tiles = [z_in[side, k * n_rows : (k + 1) * n_rows, :] for k in range(T // LANES)]
@@ -285,6 +283,8 @@
                 for z in range(2):
                     row = (side * n_rows + (c * R + r) * 2 + z) * SUB
                     ext[c, r + 1, first + z] = z_seg[row : row + SUB, :]
+    pl.when(has_hi)(lambda: start_all(out_going[1:]))
+    pl.when(has_lo)(lambda: start_all(in_going[1:]))
     for stage in range(1, len(distances) - 1):
         hear(stage)
         tell(stage + 1)

time: 17.9 us -> 19.6 us (1.095)
  the two profiles are of different devices: /device:TPU:1 before, /device:TPU:0 now
where the time goes in v5:
time: 19.6 us; the launch traced here: 19.5 us
  Pallas kernels  18.8 us (96%)
  local copies, waits for them, and re-layouts  0.65 us (3%)
    pallas_call x1, Pallas kernels, shards(): pl.pallas_call(functools.partial(kernel, n_ax, n_rad), out_shape=jax.Shap...  18.8 us
    unnamed x1, local copies, waits for them, and re-layouts  0.65 us

profile of v5, /device:TPU:0, one launch (start us, length us, event | category | flops | bytes accessed | tf_op | source)
XLA Modules:
  0.0 19.5 jit_solution(4697879115781776740)
XLA Ops:
  0.0 18.8 %shard_map.28 = f32[3,3,3,768]{3,2,1,0:T(4,128)S(1)} custom-call(f32[3,3,3,768]{3,2,1,0:T(4,128)} %v_hbm.1, s32[3,768]{1,0:T(4,128)} %map_hbm.1), custom_call_target="tpu_custom_call" | custom-call | tf_op jit(solution)/shard_map/pallas_call | solution.py:483
  18.8 0.6 %copy.4 = f32[3,3,3,768]{3,2,1,0:T(4,128)} copy(f32[3,3,3,768]{3,2,1,0:T(4,128)S(1)} %shard_map.28) | data formatting | bytes 165888

commit v6 on v4

--- a/solution.py
+++ b/solution.py
@@ -145,8 +145,13 @@
 
     greet(left, rad)
     greet(right, rad)
-    pl.when(has_lo)(lambda: greet(ax, rad - 1))
-    pl.when(has_hi)(lambda: greet(ax, rad + 1))
+
+    def greet_row(to_rad):
+        for peer in (ax, left, right):
+            greet(peer, to_rad)
+
+    pl.when(has_lo)(lambda: greet_row(rad - 1))
+    pl.when(has_hi)(lambda: greet_row(rad + 1))
 
     distances = stages(n_ax)
 
@@ -224,7 +229,7 @@
                     row = k * n_rows + (c * R + r) * 2
                     z_out[side, row : row + 2, :] = nat[c, r, first : first + 2, k * LANES : (k + 1) * LANES]
 
-    pl.semaphore_wait(barrier, 2 + jnp.where(has_lo, 1, 0) + jnp.where(has_hi, 1, 0))
+    pl.semaphore_wait(barrier, 2 + jnp.where(has_lo, 3, 0) + jnp.where(has_hi, 3, 0))
 
     def z_halo(slot, to_ax):
         return pltpu.make_async_remote_copy(
@@ -268,13 +273,11 @@
         for copy in copies:
             copy.wait_send()
 
-    pl.when(has_hi)(lambda: start_all(out_going[:1]))
-    pl.when(has_lo)(lambda: start_all(in_going[:1]))
+    pl.when(has_hi)(lambda: start_all(out_going))
+    pl.when(has_lo)(lambda: start_all(in_going))
     for stage in range(len(distances) - 1)[:1]:
         hear(stage)
         tell(stage + 1)
-    pl.when(has_hi)(lambda: start_all(out_going[1:]))
-    pl.when(has_lo)(lambda: start_all(in_going[1:]))
     for side, copy, first in ((0, z_lo, 0), (1, z_hi, Z + 2)):
         copy.wait_recv()
         tiles = [z_in[side, k * n_rows : (k + 1) * n_rows, :] for k in range(T // LANES)]

time: 17.9 us -> 17.9 us (level)
  no operation moved by 1% of the time
where the time goes in v6:
time: 17.9 us; the launch traced here: 17.8 us
  Pallas kernels  17.1 us (96%)
  local copies, waits for them, and re-layouts  0.65 us (4%)
    pallas_call x1, Pallas kernels, shards(): pl.pallas_call(functools.partial(kernel, n_ax, n_rad), out_shape=jax.Shap...  17.1 us
    unnamed x1, local copies, waits for them, and re-layouts  0.65 us

profile of v6, /device:TPU:1, one launch (start us, length us, event | category | flops | bytes accessed | tf_op | source)
XLA Modules:
  0.0 17.8 jit_solution(805852511525665946)
XLA Ops:
  0.0 17.1 %shard_map.28 = f32[3,3,3,768]{3,2,1,0:T(4,128)S(1)} custom-call(f32[3,3,3,768]{3,2,1,0:T(4,128)} %v_hbm.1, s32[3,768]{1,0:T(4,128)} %map_hbm.1), custom_call_target="tpu_custom_call" | custom-call | tf_op jit(solution)/shard_map/pallas_call | solution.py:486
  17.1 0.6 %copy.4 = f32[3,3,3,768]{3,2,1,0:T(4,128)} copy(f32[3,3,3,768]{3,2,1,0:T(4,128)S(1)} %shard_map.28) | data formatting | bytes 165888
